TPU v7x, 256 devices: a whole 4x4x8 slice. The times are simulated.
256 devices in a mesh: seq: 64 (over z, x, core), head: 4 (over y).
Axes of the slice: x: 4, y: 4, z: 8, core: 2. Of those that a mesh axis runs over, the one named last changes fastest.
Arguments:
- queries: bfloat16 [65536, 2048], P('seq', 'head'), may hold values from -14 to 14, as said below
- key_vectors: bfloat16 [65536, 2048], P('seq', 'head'), may hold values from -6 to 6
- value_vectors: bfloat16 [65536, 2048], P('seq', 'head'), may hold values from -20 to 20, as said below
- cotangent: bfloat16 [65536, 2048], P('seq', 'head'), may hold values from -6 to 6
- norm_gain: float32 [2048], P('head'), may hold values from 0.5 to 2
Outputs:
- mixed: bfloat16 [65536, 2048], P('seq', 'head')
- grad_queries: bfloat16 [65536, 2048], P('seq', 'head')
- grad_keys: bfloat16 [65536, 2048], P('seq', 'head')
- grad_values: bfloat16 [65536, 2048], P('seq', 'head')
Inputs may be any that keep to these rules, and one draw needn't show every extreme that they name: `queries`: real values. `value_vectors`: real values.
All inputs are finite; a program needn't handle non-finite values.
Results may differ from a plain program's by a relative error of at most 0.013.
Values may be sent and summed in bfloat16 or wider, within the bound.
No kernel may reach another device: no remote copies, remote signals or barrier semaphores. Data moves between devices by JAX's collectives and lax.ppermute only.
A program may use at most 128 MiB of HBM per device.

v0:
```python
import jax
import jax.numpy as jnp
from jax import lax
from jax.sharding import PartitionSpec as P

HEAD_DIM = 128
WIDTH = 2048
epsilon = 1e-06


def shards(queries, key_vectors, value_vectors, cotangent, norm_gain):
    tokens_here = queries.shape[0]
    columns = queries.shape[1]
    heads_here = columns // HEAD_DIM
    shaped_q = queries.reshape(tokens_here, heads_here, HEAD_DIM)
    shaped_k = key_vectors.reshape(tokens_here, heads_here, HEAD_DIM)
    shaped_v = value_vectors.reshape(tokens_here, heads_here, HEAD_DIM)
    block_state = jnp.einsum(
        "thd,the->hde", shaped_k, shaped_v, preferred_element_type=jnp.float32
    ).astype(jnp.bfloat16)
    position = lax.axis_index("seq")
    piece = lax.all_gather(block_state[None], "seq", axis=0, tiled=True)
    owners = jnp.arange(piece.shape[0], dtype=jnp.int32)
    select = (owners < position).astype(jnp.bfloat16)
    prefix = jnp.einsum("n,nhde->hde", select, piece, preferred_element_type=jnp.float32)
    prefix_bf = prefix.astype(jnp.bfloat16)
    causal = jnp.arange(tokens_here)[:, None] >= jnp.arange(tokens_here)[None, :]
    head_outputs = []
    head_weights = []
    for head_number in range(heads_here):
        lower = head_number * HEAD_DIM
        query_head = queries[:, lower : lower + HEAD_DIM]
        key_head = key_vectors[:, lower : lower + HEAD_DIM]
        value_head = value_vectors[:, lower : lower + HEAD_DIM]
        scores = jnp.dot(query_head, key_head.T, preferred_element_type=jnp.float32)
        weights = jnp.where(causal, scores, 0.0).astype(jnp.bfloat16)
        output = jnp.dot(weights, value_head, preferred_element_type=jnp.float32)
        output = output + jnp.dot(
            query_head, prefix_bf[head_number], preferred_element_type=jnp.float32
        )
        head_outputs.append(output)
        head_weights.append(weights)
    attn = jnp.concatenate(head_outputs, axis=1)
    upstream = cotangent.astype(jnp.float32) * norm_gain
    squares = jnp.sum(attn * attn, axis=1)
    local_dots = jnp.sum(upstream * attn, axis=1)
    square_total = lax.psum(squares, "head")
    inv = lax.rsqrt(square_total / WIDTH + epsilon)
    mixed = (attn * inv[:, None] * norm_gain).astype(jnp.bfloat16)
    dot_total = lax.psum(local_dots, "head")
    grad_attn = (
        inv[:, None] * (upstream - attn * (inv * inv * dot_total / WIDTH)[:, None])
    ).astype(jnp.bfloat16)
    grad_shaped = grad_attn.reshape(tokens_here, heads_here, HEAD_DIM)
    query_term = jnp.einsum(
        "thd,the->hde", shaped_q, grad_shaped, preferred_element_type=jnp.float32
    ).astype(jnp.bfloat16)
    piece = lax.all_gather(query_term[None], "seq", axis=0, tiled=True)
    owners = jnp.arange(piece.shape[0], dtype=jnp.int32)
    select = (owners > position).astype(jnp.bfloat16)
    suffix = jnp.einsum("n,nhde->hde", select, piece, preferred_element_type=jnp.float32)
    suffix_bf = suffix.astype(jnp.bfloat16)
    grads_q = []
    grads_k = []
    grads_v = []
    for head_number in range(heads_here):
        lower = head_number * HEAD_DIM
        query_head = queries[:, lower : lower + HEAD_DIM]
        key_head = key_vectors[:, lower : lower + HEAD_DIM]
        value_head = value_vectors[:, lower : lower + HEAD_DIM]
        grad_head = grad_attn[:, lower : lower + HEAD_DIM]
        dscores = jnp.dot(grad_head, value_head.T, preferred_element_type=jnp.float32)
        dweights = jnp.where(causal, dscores, 0.0).astype(jnp.bfloat16)
        grad_q = jnp.dot(dweights, key_head, preferred_element_type=jnp.float32)
        grad_q = grad_q + jnp.dot(
            grad_head, prefix_bf[head_number].T, preferred_element_type=jnp.float32
        )
        grad_k = jnp.dot(dweights.T, query_head, preferred_element_type=jnp.float32)
        grad_k = grad_k + jnp.dot(
            value_head, suffix_bf[head_number].T, preferred_element_type=jnp.float32
        )
        grad_v = jnp.dot(head_weights[head_number].T, grad_head, preferred_element_type=jnp.float32)
        grad_v = grad_v + jnp.dot(
            key_head, suffix_bf[head_number], preferred_element_type=jnp.float32
        )
        grads_q.append(grad_q.astype(jnp.bfloat16))
        grads_k.append(grad_k.astype(jnp.bfloat16))
        grads_v.append(grad_v.astype(jnp.bfloat16))
    return (
        mixed,
        jnp.concatenate(grads_q, axis=1),
        jnp.concatenate(grads_k, axis=1),
        jnp.concatenate(grads_v, axis=1),
    )


def solution(mesh):
    return jax.shard_map(
        shards,
        mesh=mesh,
        in_specs=(
            P("seq", "head"),
            P("seq", "head"),
            P("seq", "head"),
            P("seq", "head"),
            P("head"),
        ),
        out_specs=(P("seq", "head"), P("seq", "head"), P("seq", "head"), P("seq", "head")),
        check_vma=False,
    )
```

profile of v0, /device:TPU:1, one launch (start us, length us, event | category | flops | bytes accessed | tf_op | source)
XLA Modules:
  0.0 223.5 jit_solution(6410495051114955417)
XLA Ops:
  7.2 2.3 %copy.32 = bf16[1024,512]{0,1:T(8,128)(2,1)} copy(bf16[1024,512]{1,0:T(8,128)(2,1)} %param.6) | data formatting | bytes 2097152 | tf_op jit(solution)/shard_map/reshape | solution.py:16
  9.6 2.5 %convolution_convert_fusion.1 = bf16[4,128,128]{2,1,0:T(8,128)(2,1)} fusion(bf16[1024,4,128]{0,2,1:T(8,128)(2,1)} %bitcast.153, bf16[1024,512]{1,0:T(8,128)(2,1)S(1)} %copy-done.23), kind=kOutput, calls=%fused_computation.60 | convolution fusion | flops 134283264 | bytes 2228224 | tf_op jit(solution)/shard_map/thd,the->hde/dot_general | solution.py:18
  12.1 1.5 copy.19
  13.6 0.7 select_convert_fusion.5
  14.4 0.8 select_convert_fusion.6
  15.2 0.8 select_convert_fusion.7
  15.9 0.7 select_convert_fusion.4
  16.7 1.1 copy-done.24
  17.9 0.8 fusion.63
  18.7 1.6 fusion.75
  20.3 0.8 fusion.87
  21.2 0.8 fusion.51
  22.0 77.3 %all-gather.5.cloned.1.call-done = bf16[256,128,128]{2,1,0:T(8,128)(2,1)} async-done(((bf16[4,128,128]{2,1,0:T(8,128)(2,1)}), bf16[256,128,128]{2,1,0:T(8,128)(2,1)}) %all-gather.5.cloned.1.call-update) | async-done | bytes 8388624 | tf_op jit(solution)/shard_map/all_gather | solution.py:22
  99.3 8.1 %fusion.2 = f32[1,4,128,128]{3,0,2,1:T(1,128)S(1)} fusion(bf16[64,4,128,128]{3,2,1,0:T(8,128)(2,1)} %bitcast.150, s32[]{:T(128)S(6)} %axis_index.15), kind=kOutput, calls=%fused_computation.2 | convolution fusion | flops 8388672 | bytes 8650756 | tf_op jit(solution)/shard_map/n,nhde->hde/dot_general | solution.py:25
  107.7 0.7 copy-done.34
  110.0 8.5 %all-reduce = (f32[1024]{0:T(1024)S(1)}, f32[1024]{0:T(1024)S(1)}) all-reduce(f32[1024]{0:T(1024)S(1)} %get-tuple-element.13, f32[1024]{0:T(1024)S(1)} %get-tuple-element.12), channel_id=1, replica_groups=mesh['seq'=64,'head'=4] {'head'}, use_global_device_ids=true, to_apply=%region_1.2 | all-reduce | flops 2048 | bytes 16384 | tf_op jit(solution)/shard_map/psum | solution.py:47
  118.6 2.9 %multiply_convert_fusion = (bf16[1024,512]{0,1:T(8,128)(2,1)S(1)}, bf16[1024,512]{0,1:T(8,128)(2,1)}) fusion(bf16[1024,512]{0,1:T(8,128)(2,1)S(1)} %copy.19, f32[1024]{0:T(1024)S(1)} %get-tuple-element.18, f32[512]{0:T(512)S(1)} %copy-done.35, f32[1024]{0:T(1024)S(1)} %get-tuple-element.19, f32[1024,128]{0,1:T(8,128)} %copy-done.17, ...), kind=kLoop, calls=%fused_computation.14 | loop fusion | flops 6291456 | bytes 5253120 | tf_op jit(solution)/shard_map/convert_element_type | solution.py:53
  121.9 0.8 copy.21
  122.7 1.3 copy.22
  124.1 1.8 select_convert_fusion
  125.9 0.8 fusion.54
  127.1 0.8 select_convert_fusion.1
  127.9 0.8 fusion.66
  129.0 0.8 select_convert_fusion.2
  129.8 0.8 fusion.78
  130.9 0.8 select_convert_fusion.3
  131.7 0.8 fusion.90
  132.5 0.5 copy-done.4
  133.2 1.0 pad_maximum_fusion.1
  134.3 2.3 %copy.23 = bf16[1024,512]{1,0:T(8,128)(2,1)} copy(bf16[1024,512]{0,1:T(8,128)(2,1)} %pad_maximum_fusion.1) | data formatting | bytes 2097152
  136.6 3.0 %fusion.46 = f32[1024,128]{0,1:T(8,128)} fusion(bf16[1024,1024]{1,0:T(8,128)(2,1)} %copy-done.15, bf16[1024,512]{0,1:T(8,128)(2,1)S(1)} %get-tuple-element.16), kind=kOutput, calls=%fused_computation.82 | convolution fusion | flops 268435456 | bytes 2883584 | tf_op jit(solution)/shard_map/dot_general | solution.py:82
  139.6 1.3 fusion.42
  140.9 0.5 copy-done.10
  141.4 1.2 fusion.38
  142.6 0.5 copy-done.12
  143.2 1.2 fusion.34
  144.4 1.3 fusion.57
  145.7 0.5 copy-done.1
  146.2 0.5 fusion.69
  146.7 1.1 copy-done.3
  147.8 1.3 fusion.81
  149.6 1.3 fusion.93
  150.8 51.7 %all-gather.7.cloned.1.call-done = bf16[256,128,128]{2,1,0:T(8,128)(2,1)} async-done(((bf16[4,128,128]{2,1,0:T(8,128)(2,1)}), bf16[256,128,128]{2,1,0:T(8,128)(2,1)}) %all-gather.7.cloned.1.call-update) | async-done | bytes 8388624 | tf_op jit(solution)/shard_map/all_gather | solution.py:58
  202.6 8.1 %fusion = f32[1,4,128,128]{3,0,2,1:T(1,128)S(1)} fusion(bf16[64,4,128,128]{3,2,1,0:T(8,128)(2,1)} %bitcast.149, s32[]{:T(128)S(6)} %axis_index.15), kind=kOutput, calls=%fused_computation | convolution fusion | flops 8388672 | bytes 8650756 | tf_op jit(solution)/shard_map/n,nhde->hde/dot_general | solution.py:61
  211.2 0.5 copy-done.31
  212.3 1.3 copy.25
  214.2 0.6 copy-done.28
  215.3 1.3 copy.24
  (90 shorter events, 6.1 us)
Async XLA Ops:
  7.2 2.4 %copy-start.23 = (bf16[1024,512]{1,0:T(8,128)(2,1)S(1)}, bf16[1024,512]{1,0:T(8,128)(2,1)}, u32[]{:S(2)}) copy-start(bf16[1024,512]{1,0:T(8,128)(2,1)} %param.7) | copy-start | bytes 3145732
  7.2 92.2 %all-gather.5.cloned.1.call-start = ((), (), s32[]{:S(2)}) async-start(), calls=%async_computation | async-start | bytes 8519680 | tf_op jit(solution)/shard_map/all_gather | solution.py:22
  9.6 4.0 %copy-start.6 = (bf16[1024,512]{1,0:T(8,128)(2,1)S(1)}, bf16[1024,512]{1,0:T(8,128)(2,1)}, u32[]{:S(2)}) copy-start(bf16[1024,512]{1,0:T(8,128)(2,1)} %param.6) | copy-start | bytes 3145732
  9.6 4.0 %copy-start.19 = (bf16[1024,512]{1,0:T(8,128)(2,1)S(1)}, bf16[1024,512]{1,0:T(8,128)(2,1)}, u32[]{:S(2)}) copy-start(bf16[1024,512]{1,0:T(8,128)(2,1)} %param.5) | copy-start | bytes 3145732
  12.1 190.5 %all-gather.7.cloned.1.call-start = ((), (), s32[]{:S(2)}) async-start(), calls=%async_computation.1 | async-start | bytes 8519680 | tf_op jit(solution)/shard_map/all_gather | solution.py:58
  14.4 2.3 %copy-start.9 = (bf16[1024,1024]{1,0:T(8,128)(2,1)}, bf16[1024,1024]{1,0:T(8,128)(2,1)S(1)}, u32[]{:S(2)}) copy-start(bf16[1024,1024]{1,0:T(8,128)(2,1)S(1)} %select_convert_fusion.5) | copy-start | bytes 6291460
  15.2 3.5 %copy-start.13 = (bf16[1024,1024]{1,0:T(8,128)(2,1)}, bf16[1024,1024]{1,0:T(8,128)(2,1)S(1)}, u32[]{:S(2)}) copy-start(bf16[1024,1024]{1,0:T(8,128)(2,1)S(1)} %select_convert_fusion.6) | copy-start | bytes 6291460
  15.9 4.4 %copy-start.15 = (bf16[1024,1024]{1,0:T(8,128)(2,1)}, bf16[1024,1024]{1,0:T(8,128)(2,1)S(1)}, u32[]{:S(2)}) copy-start(bf16[1024,1024]{1,0:T(8,128)(2,1)S(1)} %select_convert_fusion.7) | copy-start | bytes 6291460
  15.9 1.9 copy-start.24
  17.9 3.3 %copy-start.11 = (bf16[1024,1024]{1,0:T(8,128)(2,1)}, bf16[1024,1024]{1,0:T(8,128)(2,1)S(1)}, u32[]{:S(2)}) copy-start(bf16[1024,1024]{1,0:T(8,128)(2,1)S(1)} %select_convert_fusion.4) | copy-start | bytes 6291460
  99.3 8.1 %copy-start.20 = (bf16[1024,512]{1,0:T(8,128)(2,1)S(1)}, bf16[1024,512]{1,0:T(8,128)(2,1)}, u32[]{:S(2)}) copy-start(bf16[1024,512]{1,0:T(8,128)(2,1)} %param.5) | copy-start | bytes 3145732
  107.4 1.0 copy-start.34
  108.4 0.8 copy-start.35
  109.0 0.8 copy-start.16
  109.2 0.8 copy-start.17
  118.6 2.9 %copy-start.21 = (bf16[1024,512]{1,0:T(8,128)(2,1)S(1)}, bf16[1024,512]{1,0:T(8,128)(2,1)}, u32[]{:S(2)}) copy-start(bf16[1024,512]{1,0:T(8,128)(2,1)} %param.5) | copy-start | bytes 3145732
  121.5 1.2 copy-start.18
  124.1 1.8 copy-start.7
  125.9 1.2 copy-start.25
  127.9 1.9 copy-start
  129.8 1.9 copy-start.2
  131.7 1.3 copy-start.4
  136.6 3.0 %copy-start.14 = (bf16[1024,1024]{1,0:T(8,128)(2,1)S(1)}, bf16[1024,1024]{1,0:T(8,128)(2,1)}, u32[]{:S(2)}) copy-start(bf16[1024,1024]{1,0:T(8,128)(2,1)} %copy-done.13) | copy-start | bytes 6291460
  139.6 1.8 copy-start.10
  141.4 1.8 copy-start.12
  143.2 1.3 copy-start.22
  144.4 1.8 copy-start.1
  146.2 1.6 copy-start.3
  147.8 1.8 copy-start.5
  202.5 8.2 %copy-start.8 = (bf16[1024,512]{1,0:T(8,128)(2,1)S(1)}, bf16[1024,512]{1,0:T(8,128)(2,1)}, u32[]{:S(2)}) copy-start(bf16[1024,512]{1,0:T(8,128)(2,1)} %param.6) | copy-start | bytes 3145732
  202.6 8.2 %copy-start.33 = (f32[1024,128]{0,1:T(8,128)S(1)}, f32[1024,128]{0,1:T(8,128)}, u32[]{:S(2)}) copy-start(f32[1024,128]{0,1:T(8,128)} %fusion.34) | copy-start | bytes 1572868
  202.6 8.4 %copy-start.32 = (f32[1024,128]{0,1:T(8,128)S(1)}, f32[1024,128]{0,1:T(8,128)}, u32[]{:S(2)}) copy-start(f32[1024,128]{0,1:T(8,128)} %fusion.38) | copy-start | bytes 1572868
  210.7 1.0 copy-start.31
  210.7 1.3 copy-start.30
  212.2 1.4 copy-start.26
  212.2 1.5 copy-start.27
  213.7 1.0 copy-start.28
  213.7 1.3 copy-start.29
Sparse Core Ops, SparseCore 0:
  12.2 87.1 all-gather.4
  122.8 79.6 all-gather.6
where the time goes:
time: 224 us; the launch traced here: 223 us
  waiting for transfers between devices  129 us (58%)
  matrix products  48.6 us (22%)
  local copies, waits for them, and re-layouts  18 us (8%)
  between operations  14.6 us (7%)
  blocking collectives  8.54 us (4%)
  other arithmetic  4.56 us (2%)
    all_gather x1, waiting for transfers between devices, shards(): piece = lax.all_gather(block_state[None], 'seq', axis=0, tiled=True)  77.3 us
    all_gather x1, waiting for transfers between devices, shards(): piece = lax.all_gather(query_term[None], 'seq', axis=0, tiled=True)  51.7 us
    dot_general x2, matrix products, shards(): jnp.einsum('n,nhde->hde', select, piece, preferred_element_type=jnp.float32)  16.2 us
    unnamed x77, local copies, waits for them, and re-layouts  14.9 us
    psum x1, blocking collectives, shards(): square_total = lax.psum(squares, 'head')  8.54 us
    dot_general x4, matrix products, shards(): jnp.dot(head_weights[head_number].T, grad_head, preferred_element_type=jn...  6.77 us
  transfers between devices with their start and end apart: 2, of which 2 were waited for; matrix products, arithmetic and copies ran while one was open for 15% of the time, Pallas kernels for 0%

commit v1 on v0

--- a/solution.py
+++ b/solution.py
@@ -19,7 +19,9 @@
         "thd,the->hde", shaped_k, shaped_v, preferred_element_type=jnp.float32
     ).astype(jnp.bfloat16)
     position = lax.axis_index("seq")
-    piece = lax.all_gather(block_state[None], "seq", axis=0, tiled=True)
+    piece = jnp.concatenate(
+        lax.all_to_all(jnp.stack([block_state[None]] * lax.axis_size("seq")), "seq", 0, 0), axis=0
+    )
     owners = jnp.arange(piece.shape[0], dtype=jnp.int32)
     select = (owners < position).astype(jnp.bfloat16)
     prefix = jnp.einsum("n,nhde->hde", select, piece, preferred_element_type=jnp.float32)

time: 224 us -> 340 us (1.52)
  waiting for transfers between devices: 129 us -> 226 us
  starting transfers between devices: 0.08 us -> 13.4 us
  local copies, waits for them, and re-layouts: 18 us -> 24.1 us
    all_to_all x0 -> x1, waiting for transfers between devices: none -> 172 us  [shards(): lax.all_to_all(jnp.stack([block_state[None]] * lax.axis_size('seq')), 'se...]
    all_gather x1 -> x0, waiting for transfers between devices: 77.3 us -> none  [shards(): piece = lax.all_gather(block_state[None], 'seq', axis=0, tiled=True)]
    all_to_all x0 -> x1, starting transfers between devices: none -> 13.2 us  [shards(): lax.all_to_all(jnp.stack([block_state[None]] * lax.axis_size('seq')), 'se...]
    another operation x0 -> x1, local copies, waits for them, and re-layouts: none -> 5.37 us  [shards(): jnp.stack([block_state[None]] * lax.axis_size('seq'))]
    unnamed x77 -> x75, local copies, waits for them, and re-layouts: 14.9 us -> 16.3 us
  transfers between devices with their start and end apart: 2 -> 2, of which waited for: 2 -> 2; matrix products, arithmetic and copies ran while one was open for 15% -> 10% of each run, Pallas kernels for 0% -> 0%
where the time goes in v1:
time: 340 us; the launch traced here: 339 us
  waiting for transfers between devices  226 us (66%)
  matrix products  47.5 us (14%)
  local copies, waits for them, and re-layouts  24.1 us (7%)
  between operations  14.6 us (4%)
  starting transfers between devices  13.4 us (4%)
  blocking collectives  9.03 us (3%)
  other arithmetic  4.57 us (1%)
    all_to_all x1, waiting for transfers between devices, shards(): lax.all_to_all(jnp.stack([block_state[None]] * lax.axis_size('seq')), 'se...  172 us
    all_gather x1, waiting for transfers between devices, shards(): piece = lax.all_gather(query_term[None], 'seq', axis=0, tiled=True)  53.8 us
    unnamed x75, local copies, waits for them, and re-layouts  16.3 us
    dot_general x2, matrix products, shards(): jnp.einsum('n,nhde->hde', select, piece, preferred_element_type=jnp.float32)  16.2 us
    all_to_all x1, starting transfers between devices, shards(): lax.all_to_all(jnp.stack([block_state[None]] * lax.axis_size('seq')), 'se...  13.2 us
    psum x1, blocking collectives, shards(): square_total = lax.psum(squares, 'head')  9.03 us
  transfers between devices with their start and end apart: 2, of which 2 were waited for; matrix products, arithmetic and copies ran while one was open for 10% of the time, Pallas kernels for 0%

profile of v1, /device:TPU:1, one launch (start us, length us, event | category | flops | bytes accessed | tf_op | source)
XLA Modules:
  0.0 338.9 jit_solution(12007786141518109728)
XLA Ops:
  7.2 1.6 copy.32
  9.2 5.4 %stack.3 = bf16[64,1,4,128,128]{4,3,2,1,0:T(8,128)(2,1)} broadcast(bf16[4,128,128]{2,1,0:T(8,128)(2,1)S(1)} %convolution_convert_fusion.1), dimensions={2,3,4} | broadcast | bytes 8519680 | tf_op jit(solution)/shard_map/stack | solution.py:23
  14.6 13.2 %all-to-all-start = ((bf16[64,1,4,128,128]{4,3,2,1,0:T(8,128)(2,1)}), bf16[64,1,4,128,128]{4,3,2,1,0:T(8,128)(2,1)}, u32[]{:S(2)}, u32[]{:S(2)}) async-start(bf16[64,1,4,128,128]{4,3,2,1,0:T(8,128)(2,1)} %stack.3), calls=%async_computation | async-start | bytes 16777216 | tf_op jit(solution)/shard_map/all_to_all | solution.py:23
  28.0 1.6 copy.19
  29.6 0.7 select_convert_fusion.4
  30.4 0.7 select_convert_fusion.5
  31.2 0.8 select_convert_fusion.6
  31.9 0.8 select_convert_fusion.7
  32.7 1.1 copy-done.23
  33.9 0.8 fusion.51
  34.7 1.6 fusion.63
  36.3 0.8 fusion.75
  37.2 0.8 fusion.87
  38.0 172.0 %all-to-all-done = bf16[64,1,4,128,128]{4,3,2,1,0:T(8,128)(2,1)} async-done(((bf16[64,1,4,128,128]{4,3,2,1,0:T(8,128)(2,1)}), bf16[64,1,4,128,128]{4,3,2,1,0:T(8,128)(2,1)}, u32[]{:S(2)}, u32[]{:S(2)}) %all-to-all-start) | async-done | bytes 8388640 | tf_op jit(solution)/shard_map/all_to_all | solution.py:23
  210.0 8.1 %fusion.2 = f32[1,4,128,128]{3,0,2,1:T(1,128)S(1)} fusion(bf16[64,4,128,128]{3,2,1,0:T(8,128)(2,1)} %bitcast.3, s32[]{:T(128)S(6)} %axis_index.15), kind=kOutput, calls=%fused_computation.2 | convolution fusion | flops 8388672 | bytes 8650756 | tf_op jit(solution)/shard_map/n,nhde->hde/dot_general | solution.py:27
  218.4 0.8 copy-done.33
  220.7 9.0 %all-reduce = (f32[1024]{0:T(1024)S(1)}, f32[1024]{0:T(1024)S(1)}) all-reduce(f32[1024]{0:T(1024)S(1)} %get-tuple-element.13, f32[1024]{0:T(1024)S(1)} %get-tuple-element.12), channel_id=1, replica_groups=mesh['seq'=64,'head'=4] {'head'}, use_global_device_ids=true, to_apply=%region_1.2 | all-reduce | flops 2048 | bytes 16384 | tf_op jit(solution)/shard_map/psum | solution.py:49
  229.8 2.9 multiply_convert_fusion
  233.1 0.8 copy.21
  233.9 1.7 select_convert_fusion.3
  235.7 1.9 fusion.90
  237.8 0.8 select_convert_fusion.2
  239.0 0.8 fusion.78
  240.1 0.8 select_convert_fusion.1
  240.9 0.8 fusion.66
  241.9 0.8 select_convert_fusion
  242.8 0.8 fusion.54
  243.6 0.5 copy-done.4
  244.4 1.0 pad_maximum_fusion.1
  245.4 2.3 copy.23
  247.7 2.3 copy.22
  250.0 3.0 fusion.46
  253.0 1.2 fusion.42
  254.2 0.5 copy-done.12
  254.7 1.3 fusion.38
  256.0 0.5 copy-done.10
  256.5 1.2 fusion.34
  257.8 1.3 fusion.93
  259.1 0.5 copy-done.1
  260.1 1.1 copy-done.3
  261.2 1.3 fusion.69
  262.4 0.5 copy-done.5
  262.9 1.3 fusion.57
  264.2 53.8 %all-gather.3.cloned.1.call-done = bf16[256,128,128]{2,1,0:T(8,128)(2,1)} async-done(((bf16[4,128,128]{2,1,0:T(8,128)(2,1)}), bf16[256,128,128]{2,1,0:T(8,128)(2,1)}) %all-gather.3.cloned.1.call-update) | async-done | bytes 8388624 | tf_op jit(solution)/shard_map/all_gather | solution.py:60
  318.0 8.1 %fusion = f32[1,4,128,128]{3,0,2,1:T(1,128)S(1)} fusion(bf16[64,4,128,128]{3,2,1,0:T(8,128)(2,1)} %bitcast.149, s32[]{:T(128)S(6)} %axis_index.15), kind=kOutput, calls=%fused_computation | convolution fusion | flops 8388672 | bytes 8650756 | tf_op jit(solution)/shard_map/n,nhde->hde/dot_general | solution.py:63
  327.8 1.3 copy.25
  329.6 0.6 copy-done.27
  330.8 1.3 copy.24
  (88 shorter events, 7.4 us)
Async XLA Ops:
  7.2 1.6 copy-start.22
  14.6 195.5 %all-to-all-start = ((bf16[64,1,4,128,128]{4,3,2,1,0:T(8,128)(2,1)}), bf16[64,1,4,128,128]{4,3,2,1,0:T(8,128)(2,1)}, u32[]{:S(2)}, u32[]{:S(2)}) async-start(bf16[64,1,4,128,128]{4,3,2,1,0:T(8,128)(2,1)} %stack.3), calls=%async_computation | async-start | bytes 16777216 | tf_op jit(solution)/shard_map/all_to_all | solution.py:23
  27.7 1.9 copy-start.6
  27.8 1.9 copy-start.18
  27.8 290.2 %all-gather.3.cloned.1.call-start = ((), (), s32[]{:S(2)}) async-start(), calls=%async_computation.1 | async-start | bytes 8519680 | tf_op jit(solution)/shard_map/all_gather | solution.py:60
  30.4 2.3 copy-start.9
  31.2 3.5 %copy-start.11 = (bf16[1024,1024]{1,0:T(8,128)(2,1)}, bf16[1024,1024]{1,0:T(8,128)(2,1)S(1)}, u32[]{:S(2)}) copy-start(bf16[1024,1024]{1,0:T(8,128)(2,1)S(1)} %select_convert_fusion.5) | copy-start | bytes 6291460
  31.9 4.4 %copy-start.13 = (bf16[1024,1024]{1,0:T(8,128)(2,1)}, bf16[1024,1024]{1,0:T(8,128)(2,1)S(1)}, u32[]{:S(2)}) copy-start(bf16[1024,1024]{1,0:T(8,128)(2,1)S(1)} %select_convert_fusion.6) | copy-start | bytes 6291460
  31.9 1.9 copy-start.23
  33.9 3.3 copy-start.15
  210.0 8.1 %copy-start.19 = (bf16[1024,512]{1,0:T(8,128)(2,1)S(1)}, bf16[1024,512]{1,0:T(8,128)(2,1)}, u32[]{:S(2)}) copy-start(bf16[1024,512]{1,0:T(8,128)(2,1)} %param.5) | copy-start | bytes 3145732
  218.1 1.0 copy-start.33
  219.1 0.8 copy-start.34
  219.6 0.8 copy-start.16
  219.9 0.8 copy-start.17
  229.8 2.9 copy-start.20
  235.6 2.1 copy-start.24
  237.8 1.2 copy-start.7
  239.0 1.9 copy-start
  240.9 1.9 copy-start.2
  242.8 1.4 copy-start.4
  250.0 3.0 copy-start.14
  253.0 1.8 copy-start.12
  254.7 1.8 copy-start.10
  256.5 1.2 copy-start.21
  257.8 1.8 copy-start.1
  259.6 1.6 copy-start.3
  261.1 1.8 copy-start.5
  318.0 8.2 %copy-start.8 = (bf16[1024,512]{1,0:T(8,128)(2,1)S(1)}, bf16[1024,512]{1,0:T(8,128)(2,1)}, u32[]{:S(2)}) copy-start(bf16[1024,512]{1,0:T(8,128)(2,1)} %param.6) | copy-start | bytes 3145732
  318.0 8.2 %copy-start.29 = (f32[1024,128]{0,1:T(8,128)S(1)}, f32[1024,128]{0,1:T(8,128)}, u32[]{:S(2)}) copy-start(f32[1024,128]{0,1:T(8,128)} %fusion.46) | copy-start | bytes 1572868
  318.0 8.4 %copy-start.30 = (f32[1024,128]{0,1:T(8,128)S(1)}, f32[1024,128]{0,1:T(8,128)}, u32[]{:S(2)}) copy-start(f32[1024,128]{0,1:T(8,128)} %fusion.42) | copy-start | bytes 1572868
  326.1 1.0 copy-start.31
  326.1 1.3 copy-start.32
  327.7 1.4 copy-start.25
  327.7 1.5 copy-start.26
  329.2 1.0 copy-start.27
  329.2 1.3 copy-start.28
Sparse Core Ops, SparseCore 0:
  234.0 83.9 all-gather.2
